TPU v7x, 256 devices: a whole 4x4x8 slice. The times are simulated.
256 devices in a mesh: row: 16 (over z, core), col: 16 (over x, y).
Axes of the slice: x: 4, y: 4, z: 8, core: 2. Of those that a mesh axis runs over, the one named last changes fastest.
Arguments:
- token_ids: int32 [32, 256], P('row'), may hold values from 0 to 16383
- passage_lengths: int32 [32], P('row'), may hold values from 64 to 256, as said below
- embedding: bfloat16 [16384, 4096], P(None, 'col'), may hold values from -8 to 8
- attn_gain: bfloat16 [4096], P('col'), may hold values from 0.25 to 1.75
- final_gain: bfloat16 [4096], P('col'), may hold values from 0.25 to 1.75
- query_weight: bfloat16 [4096, 4096], P('row', 'col'), may hold values from -0.5 to 0.5
- key_weight: bfloat16 [4096, 4096], P('row', 'col'), may hold values from -0.5 to 0.5
- value_weight: bfloat16 [4096, 4096], P('row', 'col'), may hold values from -0.09375 to 0.09375
- out_weight: bfloat16 [4096, 4096], P('row', 'col'), may hold values from -0.09375 to 0.09375
- crosskey_weight: bfloat16 [4096, 4096], P('row', 'col'), may hold values from -0.09375 to 0.09375
- crossvalue_weight: bfloat16 [4096, 4096], P('row', 'col'), may hold values from -0.09375 to 0.09375
Outputs:
- hidden_out: bfloat16 [8192, 4096], P('row', 'col')
- cross_keys: bfloat16 [8192, 16, 256], P('row', 'col')
- cross_values: bfloat16 [8192, 16, 256], P('row', 'col')
Inputs may be any that keep to these rules, and one draw needn't show every extreme that they name: `passage_lengths`: some passage of every draw has all 256 slots valid.
All inputs are finite; a program needn't handle non-finite values.
Results may differ from a plain program's by a relative error of at most 0.0082.
Values may be sent and summed in bfloat16 or wider, within the bound.
No kernel may reach another device: no remote copies, remote signals or barrier semaphores. Data moves between devices by JAX's collectives and lax.ppermute only.
A program may use at most 64 MiB of HBM per device.

v0:
```python
import jax
import jax.numpy as jnp
from jax import lax
from jax.sharding import PartitionSpec as P

D = 4096
HD = 256
PLEN = 256
epsilon = 1e-06
masked_score = -1000000000.0


def scaled_rows(widened, summed, gain_row):
    inverse = lax.rsqrt(summed / D + epsilon)
    return (widened * inverse * gain_row.astype(jnp.float32)).astype(jnp.bfloat16)


def spread_norm(row_block, gain_row, which):
    widened = row_block.astype(jnp.float32)
    partial_sum = jnp.sum(widened * widened, axis=1, keepdims=True)
    if which == 0:
        summed = lax.psum(partial_sum, "col")
        return lax.all_gather(
            scaled_rows(widened, summed, gain_row[None, :]), "col", axis=1, tiled=True
        )
    else:
        summed = lax.psum(partial_sum, "col")
        return lax.all_gather(
            scaled_rows(widened, summed, gain_row[None, :]), "col", axis=1, tiled=True
        )


def add_terms(source, pieces):
    return tuple(
        (
            jnp.dot(source, weight_piece, preferred_element_type=jnp.float32)
            for weight_piece in pieces
        )
    )


def attend(query_rows, key_rows, value_rows, passage_lengths):
    tok_rows, local_width = query_rows.shape
    passages_here = tok_rows // PLEN
    heads_here = local_width // HD
    query_four = query_rows.reshape(passages_here, PLEN, heads_here, HD)
    key_four = key_rows.reshape(passages_here, PLEN, heads_here, HD)
    value_four = value_rows.reshape(passages_here, PLEN, heads_here, HD)
    scores = jnp.einsum(
        "pihd,pjhd->phij", query_four, key_four, preferred_element_type=jnp.float32
    ) * HD ** (-0.5)
    valid = jnp.arange(PLEN, dtype=jnp.int32)[None, :] < passage_lengths[:, None]
    scores = jnp.where(valid[:, None, None, :], scores, masked_score)
    highest = jnp.max(scores, axis=-1, keepdims=True)
    expon = jnp.exp(scores - highest)
    probs = (expon / jnp.sum(expon, axis=-1, keepdims=True)).astype(jnp.bfloat16)
    mixed = jnp.einsum("phij,pjhd->pihd", probs, value_four, preferred_element_type=jnp.float32)
    return mixed.astype(jnp.bfloat16).reshape(tok_rows, local_width)


def shards(
    token_ids,
    passage_lengths,
    embedding,
    attn_gain,
    final_gain,
    query_weight,
    key_weight,
    value_weight,
    out_weight,
    crosskey_weight,
    crossvalue_weight,
):
    embedded = jnp.take(embedding, token_ids.reshape(-1), axis=0)
    normed = spread_norm(embedded, attn_gain, 0)
    tok_rows = normed.shape[0]
    local_width = query_weight.shape[1]
    query_sum, key_sum, value_sum = add_terms(
        normed,
        (
            lax.all_gather(query_weight, "row", axis=0, tiled=True),
            lax.all_gather(key_weight, "row", axis=0, tiled=True),
            lax.all_gather(value_weight, "row", axis=0, tiled=True),
        ),
    )
    attended = attend(
        query_sum.astype(jnp.bfloat16),
        key_sum.astype(jnp.bfloat16),
        value_sum.astype(jnp.bfloat16),
        passage_lengths,
    )
    heads_full = lax.all_gather(attended, "col", axis=1, tiled=True)
    (projected,) = add_terms(heads_full, (lax.all_gather(out_weight, "row", axis=0, tiled=True),))
    hidden_out = (embedded.astype(jnp.float32) + projected).astype(jnp.bfloat16)
    final_normed = spread_norm(hidden_out, final_gain, 1)
    crosskey_sum, crossvalue_sum = add_terms(
        final_normed,
        (
            lax.all_gather(crosskey_weight, "row", axis=0, tiled=True),
            lax.all_gather(crossvalue_weight, "row", axis=0, tiled=True),
        ),
    )
    heads_here = local_width // HD
    cross_keys = crosskey_sum.astype(jnp.bfloat16).reshape(tok_rows, heads_here, HD)
    cross_values = crossvalue_sum.astype(jnp.bfloat16).reshape(tok_rows, heads_here, HD)
    return (hidden_out, cross_keys, cross_values)


def solution(mesh):
    return jax.shard_map(
        shards,
        mesh=mesh,
        in_specs=(
            P("row", None),
            P("row"),
            P(None, "col"),
            P("col"),
            P("col"),
            P("row", "col"),
            P("row", "col"),
            P("row", "col"),
            P("row", "col"),
            P("row", "col"),
            P("row", "col"),
        ),
        out_specs=(P("row", "col"), P("row", "col", None), P("row", "col", None)),
        check_vma=False,
    )
```

profile of v0, /device:TPU:1, one launch (start us, length us, event | category | flops | bytes accessed | tf_op | source)
XLA Modules:
  0.0 447.0 jit_solution(17359749313425114075)
XLA Ops:
  8.6 0.7 copy.22
  9.3 6.0 %gather_fusion = bf16[512,256]{1,0:T(8,128)(2,1)S(1)} fusion(bf16[16384,256]{1,0:T(8,128)(2,1)} %param.13, s32[1024]{0:T(1024)S(1)} %pad_clamp_fusion), kind=kCustom, calls=%fused_computation | custom fusion | bytes 526336 | tf_op jit(solution)/shard_map/jit(_take)/gather | solution.py:74
  15.6 34.2 %psum.14 = f32[512,1]{0,1:T(1,128)S(1)} all-reduce(f32[512,1]{0,1:T(1,128)S(1)} %bitcast.48), channel_id=1, replica_groups=mesh['row'=16,'col'=16] {'col'}, use_global_device_ids=true, to_apply=%region_1.2 | all-reduce | flops 512 | bytes 4096 | tf_op jit(solution)/shard_map/psum | solution.py:22
  49.9 0.8 fusion.12
  52.8 0.7 all-gather.14.cloned.1.call-done
  53.5 58.8 %all-gather.10.cloned.1.call-done = bf16[512,4096]{0,1:T(8,128)(2,1)} async-done(((bf16[512,256]{0,1:T(8,128)(2,1)}), bf16[512,4096]{0,1:T(8,128)(2,1)}) %all-gather.10.cloned.1.call-update) | async-done | bytes 4194320 | tf_op jit(solution)/shard_map/all_gather | solution.py:23
  112.3 4.2 convolution_convert_fusion.4
  116.4 37.4 %all-gather.16.cloned.1.call-done = bf16[4096,256]{1,0:T(8,128)(2,1)} async-done(((bf16[256,256]{1,0:T(8,128)(2,1)}), bf16[4096,256]{1,0:T(8,128)(2,1)}) %all-gather.16.cloned.1.call-update) | async-done | bytes 2097168 | tf_op jit(solution)/shard_map/all_gather | solution.py:82
  153.9 4.2 convolution_convert_fusion.3
  158.7 34.7 %all-gather.12.cloned.1.call-done = bf16[4096,256]{1,0:T(8,128)(2,1)} async-done(((bf16[256,256]{1,0:T(8,128)(2,1)}), bf16[4096,256]{1,0:T(8,128)(2,1)}) %all-gather.12.cloned.1.call-update) | async-done | bytes 2097168 | tf_op jit(solution)/shard_map/all_gather | solution.py:83
  193.4 4.2 convolution_convert_fusion.5
  197.6 1.0 convolution_convert_fusion.2
  198.7 0.7 all-gather.24.cloned.1.call-update
  199.5 33.5 %all-gather.20.cloned.1.call-done = bf16[4096,256]{1,0:T(8,128)(2,1)} async-done(((bf16[256,256]{1,0:T(8,128)(2,1)}), bf16[4096,256]{1,0:T(8,128)(2,1)}) %all-gather.20.cloned.1.call-update) | async-done | bytes 2097168 | tf_op jit(solution)/shard_map/all_gather | solution.py:93
  232.9 61.3 %all-gather.18.cloned.1.call-done = bf16[512,4096]{1,0:T(8,128)(2,1)} async-done(((bf16[512,256]{1,0:T(8,128)(2,1)}), bf16[512,4096]{1,0:T(8,128)(2,1)}) %all-gather.18.cloned.1.call-update) | async-done | bytes 4194320 | tf_op jit(solution)/shard_map/all_gather | solution.py:92
  294.2 4.2 fusion.7
  298.4 31.3 %psum.15 = f32[512,1]{0,1:T(1,128)S(1)} all-reduce(f32[512,1]{0,1:T(1,128)S(1)} %bitcast.54), channel_id=1, replica_groups=mesh['row'=16,'col'=16] {'col'}, use_global_device_ids=true, to_apply=%region_5.6 | all-reduce | flops 512 | bytes 4096 | tf_op jit(solution)/shard_map/psum | solution.py:27
  329.7 0.8 fusion.9
  331.3 0.8 copy.19
  332.1 4.6 %all-gather.24.cloned.1.call-done = bf16[4096,256]{1,0:T(8,128)(2,1)} async-done(((bf16[256,256]{1,0:T(8,128)(2,1)}), bf16[4096,256]{1,0:T(8,128)(2,1)}) %all-gather.24.cloned.1.call-update) | async-done | bytes 2097168 | tf_op jit(solution)/shard_map/all_gather | solution.py:99
  336.7 57.3 %all-gather.22.cloned.1.call-done = bf16[512,4096]{0,1:T(8,128)(2,1)} async-done(((bf16[512,256]{0,1:T(8,128)(2,1)}), bf16[512,4096]{0,1:T(8,128)(2,1)}) %all-gather.22.cloned.1.call-update) | async-done | bytes 4194320 | tf_op jit(solution)/shard_map/all_gather | solution.py:28
  394.0 4.9 %fusion.5 = bf16[512,1,256]{2,0,1:T(8,128)(2,1)} fusion(bf16[512,4096]{0,1:T(8,128)(2,1)} %all-gather.22.cloned.1.call-done, bf16[4096,256]{1,0:T(8,128)(2,1)} %all-gather.24.cloned.1.call-done), kind=kOutput, calls=%fused_computation.14 | convolution fusion | flops 1073872896 | bytes 6553600 | tf_op jit(solution)/shard_map/dot_general | solution.py:36
  398.8 36.7 %all-gather.26.cloned.1.call-done = bf16[4096,256]{1,0:T(8,128)(2,1)} async-done(((bf16[256,256]{1,0:T(8,128)(2,1)}), bf16[4096,256]{1,0:T(8,128)(2,1)}) %all-gather.26.cloned.1.call-update) | async-done | bytes 2097168 | tf_op jit(solution)/shard_map/all_gather | solution.py:100
  435.6 4.9 %fusion.6 = bf16[512,1,256]{2,0,1:T(8,128)(2,1)} fusion(bf16[512,4096]{0,1:T(8,128)(2,1)} %all-gather.22.cloned.1.call-done, bf16[4096,256]{1,0:T(8,128)(2,1)} %all-gather.26.cloned.1.call-done), kind=kOutput, calls=%fused_computation.15 | convolution fusion | flops 1073872896 | bytes 6553600 | tf_op jit(solution)/shard_map/dot_general | solution.py:36
  (36 shorter events, 5.2 us)
Async XLA Ops:
  7.2 8.3 %copy-start = (s32[2,256]{1,0:T(2,128)S(1)}, s32[2,256]{1,0:T(2,128)}, u32[]{:S(2)}) copy-start(s32[2,256]{1,0:T(2,128)} %param.11) | copy-start | bytes 6148
  7.2 46.3 %all-gather.14.cloned.1.call-start = ((), (), s32[]{:S(2)}) async-start(), calls=%async_computation.2 | async-start | bytes 2228224 | tf_op jit(solution)/shard_map/all_gather | solution.py:81
  7.9 104.3 %all-gather.10.cloned.1.call-start = ((), (), s32[]{:S(2)}) async-start(), calls=%async_computation | async-start | bytes 4456448 | tf_op jit(solution)/shard_map/all_gather | solution.py:23
  9.3 43.4 %copy-start.1 = (s32[2]{0:T(128)S(1)}, s32[2]{0:T(128)}, u32[]{:S(2)}) copy-start(s32[2]{0:T(128)} %param.12) | copy-start | bytes 28
  50.7 103.1 %all-gather.16.cloned.1.call-start = ((), (), s32[]{:S(2)}) async-start(), calls=%async_computation.3 | async-start | bytes 2228224 | tf_op jit(solution)/shard_map/all_gather | solution.py:82
  51.5 141.9 %all-gather.12.cloned.1.call-start = ((), (), s32[]{:S(2)}) async-start(), calls=%async_computation.1 | async-start | bytes 2228224 | tf_op jit(solution)/shard_map/all_gather | solution.py:83
  52.0 180.9 %all-gather.20.cloned.1.call-start = ((), (), s32[]{:S(2)}) async-start(), calls=%async_computation.5 | async-start | bytes 2228224 | tf_op jit(solution)/shard_map/all_gather | solution.py:93
  52.6 241.6 %all-gather.18.cloned.1.call-start = ((), (), s32[]{:S(2)}) async-start(), calls=%async_computation.4 | async-start | bytes 4456448 | tf_op jit(solution)/shard_map/all_gather | solution.py:92
  197.6 1.9 copy-start.2
  198.6 138.1 %all-gather.24.cloned.1.call-start = ((), (), s32[]{:S(2)}) async-start(), calls=%async_computation.7 | async-start | bytes 2228224 | tf_op jit(solution)/shard_map/all_gather | solution.py:99
  199.4 194.6 %all-gather.22.cloned.1.call-start = ((), (), s32[]{:S(2)}) async-start(), calls=%async_computation.6 | async-start | bytes 4456448 | tf_op jit(solution)/shard_map/all_gather | solution.py:28
  330.5 105.1 %all-gather.26.cloned.1.call-start = ((), (), s32[]{:S(2)}) async-start(), calls=%async_computation.8 | async-start | bytes 2228224 | tf_op jit(solution)/shard_map/all_gather | solution.py:100
Sparse Core Ops, SparseCore 0:
  9.8 43.6 all-gather.13
  56.5 55.7 all-gather.9
  114.1 39.7 all-gather.15
  155.5 37.8 all-gather.11
  195.1 37.8 all-gather.19
  235.7 58.4 all-gather.17
  296.0 40.6 all-gather.23
  339.7 54.2 all-gather.21
  395.8 39.7 all-gather.25
where the time goes:
time: 447 us
  waiting for transfers between devices  329 us (74%)
  blocking collectives  65.5 us (15%)
  matrix products  28.1 us (6%)
  between operations  14 us (3%)
  local copies, waits for them, and re-layouts  7.71 us (2%)
    all_gather x2, waiting for transfers between devices, spread_norm(): lax.all_gather(scaled_rows(widened, summed, gain_row[None, :]), 'col', ax...  116 us
    psum x2, blocking collectives, spread_norm(): summed = lax.psum(partial_sum, 'col')  65.5 us
    all_gather x1, waiting for transfers between devices, shards(): heads_full = lax.all_gather(attended, 'col', axis=1, tiled=True)  61.3 us
    all_gather x1, waiting for transfers between devices, shards(): lax.all_gather(key_weight, 'row', axis=0, tiled=True)  37.4 us
    all_gather x1, waiting for transfers between devices, shards(): lax.all_gather(crossvalue_weight, 'row', axis=0, tiled=True)  36.7 us
    all_gather x1, waiting for transfers between devices, shards(): lax.all_gather(value_weight, 'row', axis=0, tiled=True)  34.7 us
    all_gather x1, waiting for transfers between devices, shards(): lax.all_gather(out_weight, 'row', axis=0, tiled=True)  33.5 us
    dot_general x6, matrix products, add_terms(): jnp.dot(source, weight_piece, preferred_element_type=jnp.float32)  26.4 us
  transfers between devices with their start and end apart: 9, of which 9 were waited for; matrix products, arithmetic and copies ran while one was open for 7% of the time, Pallas kernels for 0%

commit v1 on v0

--- a/solution.py
+++ b/solution.py
@@ -20,8 +20,14 @@
     partial_sum = jnp.sum(widened * widened, axis=1, keepdims=True)
     if which == 0:
         summed = lax.psum(partial_sum, "col")
-        return lax.all_gather(
-            scaled_rows(widened, summed, gain_row[None, :]), "col", axis=1, tiled=True
+        return jnp.concatenate(
+            lax.all_to_all(
+                jnp.stack([scaled_rows(widened, summed, gain_row[None, :])] * lax.axis_size("col")),
+                "col",
+                0,
+                0,
+            ),
+            axis=1,
         )
     else:
         summed = lax.psum(partial_sum, "col")

time: 447 us -> 387 us (0.87)
  waiting for transfers between devices: 329 us -> 261 us
  starting transfers between devices: 0.35 us -> 5.16 us
    all_gather x2 -> x1, waiting for transfers between devices: 116 us -> 57.3 us  [spread_norm(): lax.all_gather(scaled_rows(widened, summed, gain_row[None, :]), 'col', ax...]
    all_to_all x0 -> x1, waiting for transfers between devices: none -> 44.5 us  [spread_norm(): lax.all_to_all(jnp.stack([scaled_rows(widened, summed, gain_row[None, :])...]
    all_gather x1, waiting for transfers between devices: 37.4 us -> 0.02 us  [shards(): lax.all_gather(key_weight, 'row', axis=0, tiled=True)]
    all_gather x1, waiting for transfers between devices: 34.7 us -> 19.3 us  [shards(): lax.all_gather(value_weight, 'row', axis=0, tiled=True)]
    all_to_all x0 -> x1, starting transfers between devices: none -> 4.67 us  [spread_norm(): lax.all_to_all(jnp.stack([scaled_rows(widened, summed, gain_row[None, :])...]
  transfers between devices with their start and end apart: 9 -> 9, of which waited for: 9 -> 7; matrix products, arithmetic and copies ran while one was open for 7% -> 9% of each run, Pallas kernels for 0% -> 0%
where the time goes in v1:
time: 387 us
  waiting for transfers between devices  261 us (67%)
  blocking collectives  65.5 us (17%)
  matrix products  28.2 us (7%)
  between operations  14.2 us (4%)
  local copies, waits for them, and re-layouts  10.8 us (3%)
  starting transfers between devices  5.16 us (1%)
    psum x2, blocking collectives, spread_norm(): summed = lax.psum(partial_sum, 'col')  65.5 us
    all_gather x1, waiting for transfers between devices, shards(): heads_full = lax.all_gather(attended, 'col', axis=1, tiled=True)  61.3 us
    all_gather x1, waiting for transfers between devices, spread_norm(): lax.all_gather(scaled_rows(widened, summed, gain_row[None, :]), 'col', ax...  57.3 us
    all_to_all x1, waiting for transfers between devices, spread_norm(): lax.all_to_all(jnp.stack([scaled_rows(widened, summed, gain_row[None, :])...  44.5 us
    all_gather x1, waiting for transfers between devices, shards(): lax.all_gather(crossvalue_weight, 'row', axis=0, tiled=True)  36.7 us
    all_gather x1, waiting for transfers between devices, shards(): lax.all_gather(out_weight, 'row', axis=0, tiled=True)  33.8 us
    dot_general x6, matrix products, add_terms(): jnp.dot(source, weight_piece, preferred_element_type=jnp.float32)  26.5 us
    all_gather x1, waiting for transfers between devices, shards(): lax.all_gather(value_weight, 'row', axis=0, tiled=True)  19.3 us
  transfers between devices with their start and end apart: 9, of which 7 were waited for; matrix products, arithmetic and copies ran while one was open for 9% of the time, Pallas kernels for 0%

profile of v1, /device:TPU:1, one launch (start us, length us, event | category | flops | bytes accessed | tf_op | source)
XLA Modules:
  0.0 386.7 jit_solution(7643345845689641159)
XLA Ops:
  7.9 0.7 all-gather.13.cloned.1.call-update
  9.4 0.7 copy.23
  10.1 6.0 %gather_fusion = bf16[512,256]{1,0:T(8,128)(2,1)S(1)} fusion(bf16[16384,256]{1,0:T(8,128)(2,1)} %param.13, s32[1024]{0:T(1024)S(1)} %pad_clamp_fusion), kind=kCustom, calls=%fused_computation | custom fusion | bytes 526336 | tf_op jit(solution)/shard_map/jit(_take)/gather | solution.py:80
  16.3 0.7 copy.22
  17.7 34.2 %psum.14 = f32[512,1]{0,1:T(1,128)S(1)} all-reduce(f32[512,1]{0,1:T(1,128)S(1)} %bitcast.51), channel_id=1, replica_groups=mesh['row'=16,'col'=16] {'col'}, use_global_device_ids=true, to_apply=%region_1.2 | all-reduce | flops 512 | bytes 4096 | tf_op jit(solution)/shard_map/psum | solution.py:22
  52.1 2.4 stack.2
  54.5 4.7 %all-to-all-start = ((bf16[16,512,256]{1,2,0:T(8,128)(2,1)}), bf16[16,512,256]{1,2,0:T(8,128)(2,1)}, u32[]{:S(2)}, u32[]{:S(2)}) async-start(bf16[16,512,256]{1,2,0:T(8,128)(2,1)} %stack.2), calls=%async_computation | async-start | bytes 8388608 | tf_op jit(solution)/shard_map/all_to_all | solution.py:24
  59.8 44.5 %all-to-all-done = bf16[16,512,256]{1,2,0:T(8,128)(2,1)} async-done(((bf16[16,512,256]{1,2,0:T(8,128)(2,1)}), bf16[16,512,256]{1,2,0:T(8,128)(2,1)}, u32[]{:S(2)}, u32[]{:S(2)}) %all-to-all-start) | async-done | bytes 4194336 | tf_op jit(solution)/shard_map/all_to_all | solution.py:24
  104.4 4.2 %convolution_convert_fusion.4 = bf16[512,256]{1,0:T(8,128)(2,1)S(1)} fusion(bf16[512,4096]{0,1:T(8,128)(2,1)} %bitcast.4, bf16[4096,256]{1,0:T(8,128)(2,1)} %all-gather.11.cloned.1.call-done), kind=kOutput, calls=%fused_computation.12 | convolution fusion | flops 1073872896 | bytes 6553600 | tf_op jit(solution)/shard_map/dot_general | solution.py:42
  108.6 4.2 %convolution_convert_fusion.3 = bf16[512,256]{1,0:T(8,128)(2,1)S(1)} fusion(bf16[512,4096]{0,1:T(8,128)(2,1)} %bitcast.4, bf16[4096,256]{1,0:T(8,128)(2,1)} %all-gather.13.cloned.1.call-done), kind=kOutput, calls=%fused_computation.11 | convolution fusion | flops 1073872896 | bytes 6553600 | tf_op jit(solution)/shard_map/dot_general | solution.py:42
  113.5 19.3 %all-gather.9.cloned.1.call-done = bf16[4096,256]{1,0:T(8,128)(2,1)} async-done(((bf16[256,256]{1,0:T(8,128)(2,1)}), bf16[4096,256]{1,0:T(8,128)(2,1)}) %all-gather.9.cloned.1.call-update) | async-done | bytes 2097168 | tf_op jit(solution)/shard_map/all_gather | solution.py:89
  132.8 4.2 %convolution_convert_fusion.5 = bf16[512,256]{1,0:T(8,128)(2,1)S(1)} fusion(bf16[512,4096]{0,1:T(8,128)(2,1)} %bitcast.4, bf16[4096,256]{1,0:T(8,128)(2,1)} %all-gather.9.cloned.1.call-done), kind=kOutput, calls=%fused_computation.13 | convolution fusion | flops 1073872896 | bytes 6553600 | tf_op jit(solution)/shard_map/dot_general | solution.py:42
  137.0 1.0 convolution_convert_fusion.2
  138.7 33.8 %all-gather.17.cloned.1.call-done = bf16[4096,256]{1,0:T(8,128)(2,1)} async-done(((bf16[256,256]{1,0:T(8,128)(2,1)}), bf16[4096,256]{1,0:T(8,128)(2,1)}) %all-gather.17.cloned.1.call-update) | async-done | bytes 2097168 | tf_op jit(solution)/shard_map/all_gather | solution.py:99
  172.5 61.3 %all-gather.15.cloned.1.call-done = bf16[512,4096]{1,0:T(8,128)(2,1)} async-done(((bf16[512,256]{1,0:T(8,128)(2,1)}), bf16[512,4096]{1,0:T(8,128)(2,1)}) %all-gather.15.cloned.1.call-update) | async-done | bytes 4194320 | tf_op jit(solution)/shard_map/all_gather | solution.py:98
  233.8 4.2 %fusion.7 = (f32[512]{0:T(512)S(1)}, bf16[512,256]{0,1:T(8,128)(2,1)S(1)}) fusion(bf16[512,4096]{1,0:T(8,128)(2,1)} %all-gather.15.cloned.1.call-done, bf16[4096,256]{1,0:T(8,128)(2,1)} %all-gather.17.cloned.1.call-done, bf16[512,256]{0,1:T(8,128)(2,1)S(1)} %copy.18, pred[512]{0:T(512)(128)(4,1)S(1)} %compare_and_fusion), kind=kOutput, calls=%fused_computation.20 | convolution fusion | flops 1074658816 | bytes 6818304 | tf_op jit(solution)/shard_map/dot_general | solution.py:42
  237.9 31.3 %psum.15 = f32[512,1]{0,1:T(1,128)S(1)} all-reduce(f32[512,1]{0,1:T(1,128)S(1)} %bitcast.57), channel_id=1, replica_groups=mesh['row'=16,'col'=16] {'col'}, use_global_device_ids=true, to_apply=%region_5.6 | all-reduce | flops 512 | bytes 4096 | tf_op jit(solution)/shard_map/psum | solution.py:33
  269.2 0.8 fusion.9
  270.8 0.8 copy.20
  271.7 4.4 %all-gather.21.cloned.1.call-done = bf16[4096,256]{1,0:T(8,128)(2,1)} async-done(((bf16[256,256]{1,0:T(8,128)(2,1)}), bf16[4096,256]{1,0:T(8,128)(2,1)}) %all-gather.21.cloned.1.call-update) | async-done | bytes 2097168 | tf_op jit(solution)/shard_map/all_gather | solution.py:105
  276.1 57.3 %all-gather.19.cloned.1.call-done = bf16[512,4096]{0,1:T(8,128)(2,1)} async-done(((bf16[512,256]{0,1:T(8,128)(2,1)}), bf16[512,4096]{0,1:T(8,128)(2,1)}) %all-gather.19.cloned.1.call-update) | async-done | bytes 4194320 | tf_op jit(solution)/shard_map/all_gather | solution.py:34
  333.4 4.9 %fusion.5 = bf16[512,1,256]{2,0,1:T(8,128)(2,1)} fusion(bf16[512,4096]{0,1:T(8,128)(2,1)} %all-gather.19.cloned.1.call-done, bf16[4096,256]{1,0:T(8,128)(2,1)} %all-gather.21.cloned.1.call-done), kind=kOutput, calls=%fused_computation.14 | convolution fusion | flops 1073872896 | bytes 6553600 | tf_op jit(solution)/shard_map/dot_general | solution.py:42
  338.2 36.7 %all-gather.23.cloned.1.call-done = bf16[4096,256]{1,0:T(8,128)(2,1)} async-done(((bf16[256,256]{1,0:T(8,128)(2,1)}), bf16[4096,256]{1,0:T(8,128)(2,1)}) %all-gather.23.cloned.1.call-update) | async-done | bytes 2097168 | tf_op jit(solution)/shard_map/all_gather | solution.py:106
  375.0 4.9 %fusion.6 = bf16[512,1,256]{2,0,1:T(8,128)(2,1)} fusion(bf16[512,4096]{0,1:T(8,128)(2,1)} %all-gather.19.cloned.1.call-done, bf16[4096,256]{1,0:T(8,128)(2,1)} %all-gather.23.cloned.1.call-done), kind=kOutput, calls=%fused_computation.15 | convolution fusion | flops 1073872896 | bytes 6553600 | tf_op jit(solution)/shard_map/dot_general | solution.py:42
  (34 shorter events, 5.3 us)
Async XLA Ops:
  7.2 97.2 %all-gather.11.cloned.1.call-start = ((), (), s32[]{:S(2)}) async-start(), calls=%async_computation.2 | async-start | bytes 2228224 | tf_op jit(solution)/shard_map/all_gather | solution.py:87
  7.9 100.7 %all-gather.13.cloned.1.call-start = ((), (), s32[]{:S(2)}) async-start(), calls=%async_computation.3 | async-start | bytes 2228224 | tf_op jit(solution)/shard_map/all_gather | solution.py:88
  8.6 124.2 %all-gather.9.cloned.1.call-start = ((), (), s32[]{:S(2)}) async-start(), calls=%async_computation.1 | async-start | bytes 2228224 | tf_op jit(solution)/shard_map/all_gather | solution.py:89
  54.5 5.3 %copy-start = (s32[2]{0:T(128)S(1)}, s32[2]{0:T(128)}, u32[]{:S(2)}) copy-start(s32[2]{0:T(128)} %param.12) | copy-start | bytes 28
  54.5 49.9 %all-to-all-start = ((bf16[16,512,256]{1,2,0:T(8,128)(2,1)}), bf16[16,512,256]{1,2,0:T(8,128)(2,1)}, u32[]{:S(2)}, u32[]{:S(2)}) async-start(bf16[16,512,256]{1,2,0:T(8,128)(2,1)} %stack.2), calls=%async_computation | async-start | bytes 8388608 | tf_op jit(solution)/shard_map/all_to_all | solution.py:24
  59.1 113.3 %all-gather.17.cloned.1.call-start = ((), (), s32[]{:S(2)}) async-start(), calls=%async_computation.5 | async-start | bytes 2228224 | tf_op jit(solution)/shard_map/all_gather | solution.py:99
  59.7 174.0 %all-gather.15.cloned.1.call-start = ((), (), s32[]{:S(2)}) async-start(), calls=%async_computation.4 | async-start | bytes 4456448 | tf_op jit(solution)/shard_map/all_gather | solution.py:98
  113.5 25.2 %copy-start.1 = (bf16[256]{0:T(256)(128)(2,1)S(1)}, bf16[256]{0:T(256)(128)(2,1)}, u32[]{:S(2)}) copy-start(bf16[256]{0:T(256)(128)(2,1)} %param.15) | copy-start | bytes 1540
  138.0 138.1 %all-gather.21.cloned.1.call-start = ((), (), s32[]{:S(2)}) async-start(), calls=%async_computation.7 | async-start | bytes 2228224 | tf_op jit(solution)/shard_map/all_gather | solution.py:105
  138.6 194.8 %all-gather.19.cloned.1.call-start = ((), (), s32[]{:S(2)}) async-start(), calls=%async_computation.6 | async-start | bytes 4456448 | tf_op jit(solution)/shard_map/all_gather | solution.py:34
  270.1 104.9 %all-gather.23.cloned.1.call-start = ((), (), s32[]{:S(2)}) async-start(), calls=%async_computation.8 | async-start | bytes 2228224 | tf_op jit(solution)/shard_map/all_gather | solution.py:106
Sparse Core Ops, SparseCore 0:
  9.8 43.6 all-gather.10
  55.3 37.6 all-gather.12
  94.8 37.9 all-gather.8
  134.5 37.9 all-gather.16
  175.3 58.4 all-gather.14
  235.4 40.6 all-gather.20
  279.1 54.2 all-gather.18
  335.2 39.7 all-gather.22
